TPU v7x, 768 devices: a whole 4x8x12 slice. The times are simulated.
768 devices in a mesh: dp: 48 (over z_lo, x, core), grp: 16 (over y, z_hi).
Axes of the slice: x: 4, y: 8, z: 12 (z_hi: 2, z_lo: 6; z = z_hi * 6 + z_lo), core: 2. Of those that a mesh axis runs over, the one named last changes fastest.
Arguments:
- embeddings: bfloat16 [294912, 512], P(('dp', 'grp')), may hold values from -0.31 to 0.31
- order: int32 [768, 384], P(('dp', 'grp')), may hold values from 0 to 383, as said below
Outputs:
- emb_grad: bfloat16 [294912, 512], P(('dp', 'grp'))
- row_loss: float32 [768, 384], P(('dp', 'grp'))
Inputs may be any that keep to these rules, and one draw needn't show every extreme that they name: Each row of order is a permutation of 0 .. 383.
All inputs are finite; a program needn't handle non-finite values.
Results may differ from a plain program's by a relative error of at most 0.0046.
Values may be sent and summed in bfloat16 or wider, within the bound.
No kernel may reach another device: no remote copies, remote signals or barrier semaphores. Data moves between devices by JAX's collectives and lax.ppermute only.
A program may use at most 32 MiB of HBM per device.

v0:
```python
import jax
import jax.numpy as jnp
from jax import lax
from jax.sharding import PartitionSpec as P

K = 16


gamma = 16.0
matching_offsets = (1, 2, 3)


def passed_along(block, axis, distance):
    devices = range(lax.axis_size(axis))
    route = [((i - distance) % len(devices), i) for i in devices]
    return lax.ppermute(block, axis, route)


def on_device(embeddings, order):
    peer_count = lax.axis_size("dp")
    row_count, features = embeddings.shape
    per_peer = row_count // peer_count
    arrived = lax.all_to_all(
        embeddings.reshape(peer_count, per_peer, features),
        "dp",
        split_axis=0,
        concat_axis=0,
        tiled=True,
    )
    arrived = arrived.reshape(row_count, features)
    slots = order[0]
    owned = arrived[slots]
    owned_f = owned.astype(jnp.float32)
    inv_norm = lax.rsqrt(jnp.sum(owned_f * owned_f, axis=1, keepdims=True) + 1e-06)
    unit_f = owned_f * inv_norm
    unit_rows = unit_f.astype(jnp.bfloat16)
    partners = [passed_along(unit_rows, "grp", offset) for offset in matching_offsets]
    own_sim = jnp.dot(unit_rows, unit_rows.T, preferred_element_type=jnp.float32)
    classes = jnp.arange(row_count, dtype=jnp.int32) // K
    same_class = classes[:, None] == classes[None, :]
    diagonal = jnp.arange(row_count)[:, None] == jnp.arange(row_count)[None, :]
    positive = jnp.logical_and(same_class, jnp.logical_not(diagonal))
    negative = jnp.logical_not(same_class)
    pos_exp = jnp.where(positive, jnp.exp(-gamma * own_sim), jnp.float32(0.0))
    neg_exp = jnp.where(negative, jnp.exp(gamma * own_sim), jnp.float32(0.0))
    pos_sum = jnp.sum(pos_exp, axis=1)
    neg_sum = jnp.sum(neg_exp, axis=1)
    cross_list = []
    for partner in partners:
        cross_one = jnp.exp(
            gamma * jnp.dot(unit_rows, partner.T, preferred_element_type=jnp.float32)
        )
        neg_sum = neg_sum + jnp.sum(cross_one, axis=1)
        cross_list.append(cross_one)
    product = pos_sum * neg_sum
    row_loss = jnp.log(1.0 + product)
    weight = product / (1.0 + product)
    coef_own = (
        weight[:, None] * gamma * (neg_exp / neg_sum[:, None] - pos_exp / pos_sum[:, None])
    ).astype(jnp.bfloat16)
    own_grad = jnp.dot(coef_own, unit_rows, preferred_element_type=jnp.float32)
    own_grad = own_grad + jnp.dot(coef_own.T, unit_rows, preferred_element_type=jnp.float32)
    coef_list = []
    for partner, cross_one in zip(partners, cross_list):
        coef_one = (weight[:, None] * gamma * cross_one / neg_sum[:, None]).astype(jnp.bfloat16)
        own_grad = own_grad + jnp.dot(coef_one, partner, preferred_element_type=jnp.float32)
        coef_list.append(coef_one)
    partials = [
        jnp.dot(coef_one.T, unit_rows, preferred_element_type=jnp.float32).astype(jnp.bfloat16)
        for coef_one in coef_list
    ]
    returned_terms = [
        passed_along(partial_value, "grp", -offset)
        for partial_value, offset in zip(partials, matching_offsets)
    ]
    unit_grad = own_grad
    for term in returned_terms:
        unit_grad = unit_grad + term.astype(jnp.float32)
    owned_grad = (
        (unit_grad - unit_f * jnp.sum(unit_f * unit_grad, axis=1, keepdims=True)) * inv_norm
    ).astype(jnp.bfloat16)
    arrival_grad = jnp.zeros_like(owned_grad).at[slots].set(owned_grad)
    sent_back = lax.all_to_all(
        arrival_grad.reshape(peer_count, per_peer, features),
        "dp",
        split_axis=0,
        concat_axis=0,
        tiled=True,
    )
    return (sent_back.reshape(row_count, features), row_loss[None, :])


def solution(mesh):
    placed = (P(("dp", "grp"), None), P(("dp", "grp"), None))
    return jax.shard_map(
        on_device,
        mesh=mesh,
        in_specs=placed,
        out_specs=(P(("dp", "grp"), None), P(("dp", "grp"), None)),
        check_vma=False,
    )
```

profile of v0, /device:TPU:425, one launch (start us, length us, event | category | flops | bytes accessed | tf_op | source)
XLA Modules:
  0.0 211.8 jit_solution(13314018562936180755)
XLA Ops:
  0.6 10.5 %all-to-all-start = ((bf16[48,8,512]{2,1,0:T(8,128)(2,1)}), bf16[48,8,512]{2,1,0:T(8,128)(2,1)S(1)}, u32[]{:S(2)}, u32[]{:S(2)}) async-start(bf16[48,8,512]{2,1,0:T(8,128)(2,1)} %bitcast.25), calls=%async_computation | async-start | bytes 786432 | tf_op jit(solution)/shard_map/all_to_all | solution.py:23
  11.2 20.1 %all-to-all-done = bf16[48,8,512]{2,1,0:T(8,128)(2,1)S(1)} async-done(((bf16[48,8,512]{2,1,0:T(8,128)(2,1)}), bf16[48,8,512]{2,1,0:T(8,128)(2,1)S(1)}, u32[]{:S(2)}, u32[]{:S(2)}) %all-to-all-start) | async-done | bytes 393248 | tf_op jit(solution)/shard_map/all_to_all | solution.py:23
  31.3 2.1 gather_fusion
  33.4 0.2 fusion.15
  33.5 0.1 fusion.10
  33.7 1.9 collective-permute-start
  35.6 9.9 %collective-permute-start.2 = (bf16[384,512]{1,0:T(8,128)(2,1)S(1)}, bf16[384,512]{1,0:T(8,128)(2,1)S(1)}, u32[]{:S(2)}, u32[]{:S(2)}) collective-permute-start(bf16[384,512]{1,0:T(8,128)(2,1)S(1)} %fusion.10), channel_id=1, source_target_pairs={{13,0},{14,1},{15,2},{0,3},{1,4},{2,5},{3,6},{4,7},{5,8},{6,9},{7,... | collective-permute-start | bytes 1179656 | tf_op jit(solution)/shard_map/ppermute | solution.py:16
  45.5 1.9 collective-permute-start.1
  47.5 0.6 fusion.22
  48.0 21.4 %collective-permute-done = bf16[384,512]{1,0:T(8,128)(2,1)S(1)} collective-permute-done((bf16[384,512]{1,0:T(8,128)(2,1)S(1)}, bf16[384,512]{1,0:T(8,128)(2,1)S(1)}, u32[]{:S(2)}, u32[]{:S(2)}) %collective-permute-start) | collective-permute-done | bytes 393248 | tf_op jit(solution)/shard_map/ppermute | solution.py:16
  69.4 0.4 fusion.34
  69.8 0.4 fusion.33
  70.2 18.2 %collective-permute-done.2 = bf16[384,512]{1,0:T(8,128)(2,1)S(1)} collective-permute-done((bf16[384,512]{1,0:T(8,128)(2,1)S(1)}, bf16[384,512]{1,0:T(8,128)(2,1)S(1)}, u32[]{:S(2)}, u32[]{:S(2)}) %collective-permute-start.2) | collective-permute-done | bytes 393248 | tf_op jit(solution)/shard_map/ppermute | solution.py:16
  88.5 0.4 fusion.32
  88.9 0.4 convolution_convert_fusion
  89.3 0.4 convolution_convert_fusion.1
  89.7 0.4 convolution_convert_fusion.2
  90.1 4.3 %collective-permute-start.3 = (bf16[384,512]{1,0:T(8,128)(2,1)S(1)}, bf16[384,512]{1,0:T(8,128)(2,1)S(1)}, u32[]{:S(2)}, u32[]{:S(2)}) collective-permute-start(bf16[384,512]{1,0:T(8,128)(2,1)S(1)} %convolution_convert_fusion.2), channel_id=1, source_target_pairs={{1,0},{2,1},{3,2},{4,3},{5,4},{6,5},{7,6},{8,7},{9,8},{10,9},{11,1... | collective-permute-start | bytes 1179656 | tf_op jit(solution)/shard_map/ppermute | solution.py:16
  94.4 1.9 collective-permute-start.4
  96.3 1.9 collective-permute-start.5
  98.3 0.7 fusion.31
  98.9 0.4 fusion.30
  99.3 0.4 fusion.29
  99.8 0.6 convolution_add_fusion.1
  100.3 23.5 %collective-permute-done.3 = bf16[384,512]{1,0:T(8,128)(2,1)S(1)} collective-permute-done((bf16[384,512]{1,0:T(8,128)(2,1)S(1)}, bf16[384,512]{1,0:T(8,128)(2,1)S(1)}, u32[]{:S(2)}, u32[]{:S(2)}) %collective-permute-start.3) | collective-permute-done | bytes 393248 | tf_op jit(solution)/shard_map/ppermute | solution.py:16
  123.8 26.0 %collective-permute-done.5 = bf16[384,512]{1,0:T(8,128)(2,1)S(1)} collective-permute-done((bf16[384,512]{1,0:T(8,128)(2,1)S(1)}, bf16[384,512]{1,0:T(8,128)(2,1)S(1)}, u32[]{:S(2)}, u32[]{:S(2)}) %collective-permute-start.5) | collective-permute-done | bytes 393248 | tf_op jit(solution)/shard_map/ppermute | solution.py:16
  149.8 0.7 fusion.11
  150.5 2.8 %scatter_custom_fusion = bf16[384,512]{1,0:T(8,128)(2,1)} fusion(s32[384]{0:T(512)S(1)} %fusion.28, f32[384,512]{1,0:T(8,128)S(1)} %get-tuple-element.14, bf16[384,512]{1,0:T(8,128)(2,1)S(1)} %gather_fusion, f32[384]{0:T(512)S(1)} %get-tuple-element.13, f32[384]{0:T(512)S(1)} %add_rsqrt_fusion, bf16[]{:T(256)} %constant.24.clone.1), kind=kCustom, calls=%fused_computation.38 | custom fusion | flops 1179648 | bytes 1576962 | tf_op jit(solution)/shard_map/scatter | solution.py:82
  153.3 37.5 %all-to-all-start.1 = ((bf16[48,8,512]{2,1,0:T(8,128)(2,1)}), bf16[48,8,512]{2,1,0:T(8,128)(2,1)S(1)}, u32[]{:S(2)}, u32[]{:S(2)}) async-start(bf16[48,8,512]{2,1,0:T(8,128)(2,1)} %bitcast.3), calls=%async_computation.1 | async-start | bytes 786432 | tf_op jit(solution)/shard_map/all_to_all | solution.py:83
  190.9 0.6 reshape.152
  191.4 19.6 %all-to-all-done.1 = bf16[48,8,512]{2,1,0:T(8,128)(2,1)S(1)} async-done(((bf16[48,8,512]{2,1,0:T(8,128)(2,1)}), bf16[48,8,512]{2,1,0:T(8,128)(2,1)S(1)}, u32[]{:S(2)}, u32[]{:S(2)}) %all-to-all-start.1) | async-done | bytes 393248 | tf_op jit(solution)/shard_map/all_to_all | solution.py:83
  211.0 0.7 copy.5
  (10 shorter events, 0.1 us)
Async XLA Ops:
  0.6 10.5 %copy-start = (s32[1,384]{1,0:T(1,128)S(1)}, s32[1,384]{1,0:T(1,128)}, u32[]{:S(2)}) copy-start(s32[1,384]{1,0:T(1,128)} %param.3) | copy-start | bytes 4612
  0.6 30.7 %all-to-all-start = ((bf16[48,8,512]{2,1,0:T(8,128)(2,1)}), bf16[48,8,512]{2,1,0:T(8,128)(2,1)S(1)}, u32[]{:S(2)}, u32[]{:S(2)}) async-start(bf16[48,8,512]{2,1,0:T(8,128)(2,1)} %bitcast.25), calls=%async_computation | async-start | bytes 786432 | tf_op jit(solution)/shard_map/all_to_all | solution.py:23
  33.7 35.7 %collective-permute-start = (bf16[384,512]{1,0:T(8,128)(2,1)S(1)}, bf16[384,512]{1,0:T(8,128)(2,1)S(1)}, u32[]{:S(2)}, u32[]{:S(2)}) collective-permute-start(bf16[384,512]{1,0:T(8,128)(2,1)S(1)} %fusion.10), channel_id=1, source_target_pairs={{15,0},{0,1},{1,2},{2,3},{3,4},{4,5},{5,6},{6,7},{7,8},{8,9},{9,10... | collective-permute-start | bytes 1179656 | tf_op jit(solution)/shard_map/ppermute | solution.py:16
  35.6 52.8 %collective-permute-start.2 = (bf16[384,512]{1,0:T(8,128)(2,1)S(1)}, bf16[384,512]{1,0:T(8,128)(2,1)S(1)}, u32[]{:S(2)}, u32[]{:S(2)}) collective-permute-start(bf16[384,512]{1,0:T(8,128)(2,1)S(1)} %fusion.10), channel_id=1, source_target_pairs={{13,0},{14,1},{15,2},{0,3},{1,4},{2,5},{3,6},{4,7},{5,8},{6,9},{7,... | collective-permute-start | bytes 1179656 | tf_op jit(solution)/shard_map/ppermute | solution.py:16
  45.5 24.3 %collective-permute-start.1 = (bf16[384,512]{1,0:T(8,128)(2,1)S(1)}, bf16[384,512]{1,0:T(8,128)(2,1)S(1)}, u32[]{:S(2)}, u32[]{:S(2)}) collective-permute-start(bf16[384,512]{1,0:T(8,128)(2,1)S(1)} %fusion.10), channel_id=1, source_target_pairs={{14,0},{15,1},{0,2},{1,3},{2,4},{3,5},{4,6},{5,7},{6,8},{7,9},{8,1... | collective-permute-start | bytes 1179656 | tf_op jit(solution)/shard_map/ppermute | solution.py:16
  90.1 33.7 %collective-permute-start.3 = (bf16[384,512]{1,0:T(8,128)(2,1)S(1)}, bf16[384,512]{1,0:T(8,128)(2,1)S(1)}, u32[]{:S(2)}, u32[]{:S(2)}) collective-permute-start(bf16[384,512]{1,0:T(8,128)(2,1)S(1)} %convolution_convert_fusion.2), channel_id=1, source_target_pairs={{1,0},{2,1},{3,2},{4,3},{5,4},{6,5},{7,6},{8,7},{9,8},{10,9},{11,1... | collective-permute-start | bytes 1179656 | tf_op jit(solution)/shard_map/ppermute | solution.py:16
  94.4 29.4 %collective-permute-start.4 = (bf16[384,512]{1,0:T(8,128)(2,1)S(1)}, bf16[384,512]{1,0:T(8,128)(2,1)S(1)}, u32[]{:S(2)}, u32[]{:S(2)}) collective-permute-start(bf16[384,512]{1,0:T(8,128)(2,1)S(1)} %convolution_convert_fusion.1), channel_id=1, source_target_pairs={{2,0},{3,1},{4,2},{5,3},{6,4},{7,5},{8,6},{9,7},{10,8},{11,9},{12,... | collective-permute-start | bytes 1179656 | tf_op jit(solution)/shard_map/ppermute | solution.py:16
  96.3 53.5 %collective-permute-start.5 = (bf16[384,512]{1,0:T(8,128)(2,1)S(1)}, bf16[384,512]{1,0:T(8,128)(2,1)S(1)}, u32[]{:S(2)}, u32[]{:S(2)}) collective-permute-start(bf16[384,512]{1,0:T(8,128)(2,1)S(1)} %convolution_convert_fusion), channel_id=1, source_target_pairs={{3,0},{4,1},{5,2},{6,3},{7,4},{8,5},{9,6},{10,7},{11,8},{12,9},{13... | collective-permute-start | bytes 1179656 | tf_op jit(solution)/shard_map/ppermute | solution.py:16
  153.3 57.7 %all-to-all-start.1 = ((bf16[48,8,512]{2,1,0:T(8,128)(2,1)}), bf16[48,8,512]{2,1,0:T(8,128)(2,1)S(1)}, u32[]{:S(2)}, u32[]{:S(2)}) async-start(bf16[48,8,512]{2,1,0:T(8,128)(2,1)} %bitcast.3), calls=%async_computation.1 | async-start | bytes 786432 | tf_op jit(solution)/shard_map/all_to_all | solution.py:83
where the time goes:
time: 212 us
  waiting for transfers between devices  129 us (61%)
  starting transfers between devices  69.9 us (33%)
  matrix products  5.69 us (3%)
  local copies, waits for them, and re-layouts  3.37 us (2%)
  other arithmetic  3.19 us (2%)
    ppermute x6, waiting for transfers between devices, passed_along(): return lax.ppermute(block, axis, route)  89.1 us
    all_to_all x1, starting transfers between devices, on_device(): lax.all_to_all(arrival_grad.reshape(peer_count, per_peer, features), 'dp'...  37.5 us
    ppermute x6, starting transfers between devices, passed_along(): return lax.ppermute(block, axis, route)  21.9 us
    all_to_all x1, waiting for transfers between devices, on_device(): lax.all_to_all(embeddings.reshape(peer_count, per_peer, features), 'dp',...  20.1 us
    all_to_all x1, waiting for transfers between devices, on_device(): lax.all_to_all(arrival_grad.reshape(peer_count, per_peer, features), 'dp'...  19.6 us
    all_to_all x1, starting transfers between devices, on_device(): lax.all_to_all(embeddings.reshape(peer_count, per_peer, features), 'dp',...  10.5 us
  transfers between devices with their start and end apart: 8, of which 6 were waited for; matrix products, arithmetic and copies ran while one was open for 2% of the time, Pallas kernels for 0%

commit v1 on v0

v1 whole, which is shorter than its diff:
```python
import functools

import jax
import jax.numpy as jnp
import numpy as np
from jax import lax
from jax.experimental import pallas as pl
from jax.experimental.pallas import tpu as pltpu
from jax.sharding import Mesh
from jax.sharding import PartitionSpec as P

K = 16
gamma = 16.0
F32 = jnp.float32
BF16 = jnp.bfloat16
WHERE = ("zl", "x", "zh")


def rows_by_rows(a, b):
    return lax.dot_general(a, b, (((1,), (1,)), ((), ())), preferred_element_type=F32)


def cols_by_cols(a, b):
    return lax.dot_general(a, b, (((0,), (0,)), ((), ())), preferred_element_type=F32)


def row_ids(half, core, shape, axis):
    i = lax.broadcasted_iota(jnp.int32, shape, axis)
    return (i // 8) * 16 + core * 8 + i % 8


def pick_orders(core, mine, other):
    first = core == 0
    return jnp.where(first, mine, other), jnp.where(first, other, mine)


def pack_kernel(core_ref, x_ref, mine_ref, other_ref, full_ref, a_ref, b_ref):
    core = core_ref[0]
    half = a_ref.shape[0] - 8
    rows = mine_ref.shape[1]
    features = x_ref.shape[-1]
    slot_class = (lax.broadcasted_iota(jnp.int32, (8, rows), 1) // K).astype(BF16)
    orders = pick_orders(core, mine_ref[...], other_ref[...])
    ids = row_ids(half, core, (half, rows), 0)
    labels = []
    for order in orders:
        chosen = jnp.where(ids == order, 1.0, 0.0).astype(BF16)
        labels.append(rows_by_rows(slot_class, chosen))
    tile = jnp.zeros((8, features), F32)
    room = features // 2
    gap = jnp.zeros((8, room - half), F32)
    tile = jnp.concatenate([labels[0], gap, labels[1], gap], axis=1).astype(BF16)
    for which in range(2):
        x = x_ref[:, which].astype(F32).reshape(half, features)
        inv = lax.rsqrt(jnp.sum(x * x, axis=1, keepdims=True) + 1e-06)
        unit = (x * inv).astype(BF16)
        if which == 0:
            full_ref[0:half] = unit
            a_ref[0:half] = unit
        else:
            full_ref[half + 8 :] = unit
            b_ref[...] = unit
    full_ref[half : half + 8] = tile
    a_ref[half : half + 8] = tile


def loss_kernel(
    core_ref, x_ref, mine_ref, other_ref,
    y0_ref, y0o_ref, dn_ref, dno_ref, up_ref, upo_ref, dn2_ref, dn2o_ref, up2_ref, up2o_ref,
    grad_ref, loss_ref, w, coef_rows, coef_cols,
):
    core = core_ref[0]
    half = dn2_ref.shape[0]
    rows = 2 * half
    features = x_ref.shape[-1]
    room = features // 2
    second = half + 8

    def place(block, own, other, start):
        w[block * rows : block * rows + half] = own[start : start + half]
        w[block * rows + half : (block + 1) * rows] = other[start : start + half]

    place(0, dn2_ref, dn2o_ref, 0)
    place(1, dn_ref, dno_ref, 0)
    place(2, dn_ref, dno_ref, second)
    place(3, y0_ref, y0o_ref, 0)
    place(4, y0_ref, y0o_ref, second)
    place(5, up_ref, upo_ref, 0)
    place(6, up_ref, upo_ref, second)
    place(7, up2_ref, up2o_ref, 0)

    def labels_of(own, other, which):
        lanes = slice(which * room, which * room + half)
        return jnp.concatenate(
            [own[half:second, lanes].astype(F32), other[half:second, lanes].astype(F32)], axis=1
        )[0:1]

    label_rows = {
        3: labels_of(y0_ref, y0o_ref, 0),
        4: labels_of(y0_ref, y0o_ref, 1),
        5: labels_of(up_ref, upo_ref, 0),
        6: labels_of(up_ref, upo_ref, 1),
        7: labels_of(up2_ref, up2o_ref, 0),
    }
    kinds = -(-(rows // K) // 16) * 16
    kind = lax.broadcasted_iota(jnp.int32, (kinds, rows), 0).astype(F32)
    diagonal = lax.broadcasted_iota(jnp.int32, (rows, rows), 0) == lax.broadcasted_iota(
        jnp.int32, (rows, rows), 1
    )
    losses = []
    for i in range(3, 8):
        anchor = w[i * rows : (i + 1) * rows]
        one_hot = jnp.where(kind == label_rows[i], 1.0, 0.0).astype(BF16)
        same = cols_by_cols(one_hot, one_hot) > 0.5
        own = rows_by_rows(anchor, anchor)
        e_own = jnp.exp(gamma * jnp.where(same, -own, own))
        pos = jnp.where(jnp.logical_and(same, jnp.logical_not(diagonal)), e_own, 0.0)
        neg = jnp.where(same, 0.0, e_own)
        pos_sum = jnp.sum(pos, axis=1, keepdims=True)
        neg_sum = jnp.sum(neg, axis=1, keepdims=True)
        cross = jnp.exp(gamma * rows_by_rows(anchor, w[(i - 3) * rows : i * rows]))
        neg_sum = neg_sum + jnp.sum(cross, axis=1, keepdims=True)
        product = pos_sum * neg_sum
        weight = product / (1.0 + product)
        on_neg = gamma * weight / neg_sum
        on_pos = gamma * weight / pos_sum
        coef_own = (on_neg * neg - on_pos * pos).astype(BF16)
        if i < 5:
            losses.append(jnp.log(1.0 + product))
            mine = i - 3
            coef_rows[mine, :, 0 : 3 * rows] = (on_neg[0:half] * cross[0:half]).astype(BF16)
            coef_rows[mine, :, 3 * rows :] = coef_own[0:half]
        for target in (3, 4):
            if target == i:
                part = coef_own[:, 0:half]
            elif i - 3 <= target < i:
                lane = (target - (i - 3)) * rows
                part = (on_neg * cross[:, lane : lane + half]).astype(BF16)
            else:
                continue
            first = (i - target) * rows
            coef_cols[target - 3, first : first + rows] = part

    for which in range(2):
        total = jnp.dot(
            coef_rows[which], w[which * rows : (which + 4) * rows], preferred_element_type=F32
        )
        total = total + cols_by_cols(
            coef_cols[which], w[(which + 3) * rows : (which + 7) * rows]
        )
        x = x_ref[:, which].astype(F32).reshape(half, features)
        inv = lax.rsqrt(jnp.sum(x * x, axis=1, keepdims=True) + 1e-06)
        u = x * inv
        grad = (total - u * jnp.sum(u * total, axis=1, keepdims=True)) * inv
        grad_ref[:, which] = grad.reshape(half // 8, 8, features).astype(BF16)

    ids = jnp.concatenate(
        [row_ids(half, core, (half, rows), 0), row_ids(half, 1 - core, (half, rows), 0)], axis=0
    )
    orders = pick_orders(core, mine_ref[...], other_ref[...])
    by_slot = [
        jnp.sum(jnp.where(ids == order, loss, 0.0), axis=0, keepdims=True)
        for order, loss in zip(orders, losses)
    ]
    loss_ref[...] = jnp.where(core == 0, by_slot[0], by_slot[1])


VMEM = pl.BlockSpec(memory_space=pltpu.VMEM)
SMEM = pl.BlockSpec(memory_space=pltpu.SMEM)


def on_device(embeddings, order):
    rows, features = embeddings.shape
    peers = lax.axis_size(WHERE)
    per_peer = rows // peers
    half = rows // 2
    core = lax.axis_index("c").astype(jnp.int32).reshape(1)
    ring = lax.axis_size("y")

    turned = [(c * 2 + h, h * 2 + c) for h in range(2) for c in range(2)]
    crossed = [(c * 2 + h, (1 - h) * 2 + c) for h in range(2) for c in range(2)]
    mine = lax.ppermute(order, ("c", "zh"), turned)
    other = lax.ppermute(order, ("c", "zh"), crossed)

    def swap_cores(value):
        return lax.ppermute(value, "c", [(0, 1), (1, 0)])

    def along(value, distance):
        return lax.ppermute(value, "y", [(i, (i + distance) % ring) for i in range(ring)])

    arrived = lax.all_to_all(
        embeddings.reshape(peers, per_peer, features), WHERE, 0, 0, tiled=True
    ).reshape(peers // 2, 2, per_peer, features)

    full, part_a, part_b = pl.pallas_call(
        pack_kernel,
        out_shape=(
            jax.ShapeDtypeStruct((rows + 8, features), BF16),
            jax.ShapeDtypeStruct((half + 8, features), BF16),
            jax.ShapeDtypeStruct((half, features), BF16),
        ),
        in_specs=[SMEM, VMEM, VMEM, VMEM],
        out_specs=(VMEM, VMEM, VMEM),
        name="pack",
        cost_estimate=pl.CostEstimate(flops=10**7, bytes_accessed=10**6, transcendentals=0),
    )(core, arrived, mine, other)

    down = along(full, 1)
    up = along(full, -1)
    down2 = along(part_b, 2)
    up2 = along(part_a, -2)
    full_o = swap_cores(full)
    down_o = swap_cores(down)
    up_o = swap_cores(up)
    down2_o = swap_cores(down2)
    up2_o = swap_cores(up2)

    grad, loss = pl.pallas_call(
        loss_kernel,
        out_shape=(
            jax.ShapeDtypeStruct((peers // 2, 2, per_peer, features), BF16),
            jax.ShapeDtypeStruct((1, rows), F32),
        ),
        in_specs=[SMEM] + [VMEM] * 13,
        out_specs=(VMEM, VMEM),
        scratch_shapes=[
            pltpu.VMEM((8 * rows, features), BF16),
            pltpu.VMEM((2, half, 4 * rows), BF16),
            pltpu.VMEM((2, 4 * rows, half), BF16),
        ],
        name="loss_and_grad",
        cost_estimate=pl.CostEstimate(
            flops=4 * 10**9, bytes_accessed=10**7, transcendentals=3 * 10**6
        ),
    )(
        core, arrived, mine, other, full, full_o, down, down_o, up, up_o, down2, down2_o, up2, up2_o
    )

    row_loss = lax.ppermute(loss, ("c", "zh"), turned)
    sent_back = lax.all_to_all(
        grad.reshape(peers, per_peer, features), WHERE, 0, 0, tiled=True
    )
    return sent_back.reshape(rows, features), row_loss


def solution(mesh):
    dp, grp = mesh.devices.shape
    zl, x = SPLIT.get((dp, grp), (6, 4))
    parts = Mesh(
        mesh.devices.reshape(zl, x, 2, grp // 2, 2), ("zl", "x", "c", "y", "zh")
    )
    placed = P(("zl", "x", "c", "y", "zh"), None)
    return jax.shard_map(
        on_device, mesh=parts, in_specs=(placed, placed), out_specs=(placed, placed), check_vma=False
    )


SPLIT = {(48, 16): (6, 4)}
```

time: 212 us -> 126 us (0.59)
  the two profiles are of different devices: /device:TPU:425 before, /device:TPU:8 now
where the time goes in v1:
time: 126 us; the launch traced here: 125 us
  starting transfers between devices  54.5 us (43%)
  waiting for transfers between devices  54.1 us (43%)
  Pallas kernels  11.1 us (9%)
  local copies, waits for them, and re-layouts  4.35 us (3%)
    all_to_all x1, waiting for transfers between devices, on_device(): lax.all_to_all(grad.reshape(peers, per_peer, features), WHERE, 0, 0, tile...  20.8 us
    all_to_all x1, starting transfers between devices, on_device(): lax.all_to_all(embeddings.reshape(peers, per_peer, features), WHERE, 0, 0...  18.3 us
    ppermute x1, waiting for transfers between devices, on_device(): other = lax.ppermute(order, ('c', 'zh'), crossed)  18.1 us
    ppermute x4, starting transfers between devices, along(): lax.ppermute(value, 'y', [(i, (i + distance) % ring) for i in range(ring)])  18 us
    ppermute x4, waiting for transfers between devices, along(): lax.ppermute(value, 'y', [(i, (i + distance) % ring) for i in range(ring)])  12.7 us
    ppermute x5, starting transfers between devices, swap_cores(): return lax.ppermute(value, 'c', [(0, 1), (1, 0)])  10.1 us
    pallas_call x1, Pallas kernels, on_device(): pl.pallas_call(loss_kernel, out_shape=(jax.ShapeDtypeStruct((peers // 2,...  8.92 us
    all_to_all x1, starting transfers between devices, on_device(): lax.all_to_all(grad.reshape(peers, per_peer, features), WHERE, 0, 0, tile...  4.93 us
  transfers between devices with their start and end apart: 14, of which 6 were waited for; matrix products, arithmetic and copies ran while one was open for 0% of the time, Pallas kernels for 0%

profile of v1, /device:TPU:8, one launch (start us, length us, event | category | flops | bytes accessed | tf_op | source)
XLA Modules:
  0.0 124.9 jit_solution(12791499050442555934)
XLA Ops:
  0.6 18.3 %all-to-all-start = ((bf16[48,8,512]{2,1,0:T(8,128)(2,1)}), bf16[48,8,512]{2,1,0:T(8,128)(2,1)S(1)}, u32[]{:S(2)}, u32[]{:S(2)}) async-start(bf16[48,8,512]{2,1,0:T(8,128)(2,1)} %bitcast.8), calls=%async_computation | async-start | bytes 786432 | tf_op jit(solution)/shard_map/all_to_all | solution.py:191
  19.0 1.9 %collective-permute-start.1 = (s32[1,384]{1,0:T(1,128)S(1)}, s32[1,384]{1,0:T(1,128)S(1)}, u32[]{:S(2)}, u32[]{:S(2)}) collective-permute-start(s32[1,384]{1,0:T(1,128)S(1)} %copy-done.12), channel_id=1, source_target_pairs={{0,16},{16,17},{1,0},{17,1},{2,18},{18,19},{3,2},{19,3},{4,20},{20... | collective-permute-start | bytes 4616 | tf_op jit(solution)/shard_map/ppermute | solution.py:183
  20.9 0.7 collective-permute-start
  21.6 18.1 %collective-permute-done.1.other_ref = s32[1,384]{1,0:T(1,128)S(1)} collective-permute-done((s32[1,384]{1,0:T(1,128)S(1)}, s32[1,384]{1,0:T(1,128)S(1)}, u32[]{:S(2)}, u32[]{:S(2)}) %collective-permute-start.1) | collective-permute-done | bytes 1568 | tf_op jit(solution)/shard_map/ppermute | solution.py:183
  39.6 0.0 collective-permute-done.mine_ref
  39.6 1.1 all-to-all-done
  40.7 0.7 copy-done
  41.5 2.1 %pack.1 = (bf16[392,512]{1,0:T(8,128)(2,1)}, bf16[200,512]{1,0:T(8,128)(2,1)}, bf16[192,512]{1,0:T(8,128)(2,1)}) custom-call(s32[1]{0:T(128)} %bitcast.core_ref, bf16[24,2,8,512]{3,2,1,0:T(8,128)(2,1)} %bitcast.5, s32[1,384]{1,0:T(1,128)} %copy-done.2, s32[1,384]{1,0:T(1,128)} %copy-done.1), custom_call_target="tpu_custom_call" | custom-call | flops 10000000 | bytes 1000000 | tf_op jit(solution)/shard_map/pack/pallas_call | solution.py:195
  43.6 2.3 %collective-permute-start.5 = (bf16[392,512]{1,0:T(8,128)(2,1)}, bf16[392,512]{1,0:T(8,128)(2,1)S(1)}, u32[]{:S(2)}, u32[]{:S(2)}) collective-permute-start(bf16[392,512]{1,0:T(8,128)(2,1)} %get-tuple-element.7.y0_ref), channel_id=1, source_target_pairs={{0,14},{2,0},{4,2},{6,4},{8,6},{10,8},{12,10},{14,12},{1,15},{3,1}... | collective-permute-start | bytes 1204232 | tf_op jit(solution)/shard_map/ppermute | solution.py:189
  46.0 3.5 %collective-permute-start.3 = (bf16[392,512]{1,0:T(8,128)(2,1)}, bf16[392,512]{1,0:T(8,128)(2,1)S(1)}, u32[]{:S(2)}, u32[]{:S(2)}) collective-permute-start(bf16[392,512]{1,0:T(8,128)(2,1)} %get-tuple-element.7.y0_ref), channel_id=1, source_target_pairs={{0,2},{2,4},{4,6},{6,8},{8,10},{10,12},{12,14},{14,0},{1,3},{3,5},... | collective-permute-start | bytes 1204232 | tf_op jit(solution)/shard_map/ppermute | solution.py:189
  49.5 6.5 %collective-permute-start.9 = (bf16[200,512]{1,0:T(8,128)(2,1)}, bf16[200,512]{1,0:T(8,128)(2,1)S(1)}, u32[]{:S(2)}, u32[]{:S(2)}) collective-permute-start(bf16[200,512]{1,0:T(8,128)(2,1)} %get-tuple-element.9), channel_id=1, source_target_pairs={{0,12},{2,14},{4,0},{6,2},{8,4},{10,6},{12,8},{14,10},{1,13},{3,15... | collective-permute-start | bytes 614408 | tf_op jit(solution)/shard_map/ppermute | solution.py:189
  55.9 1.9 %collective-permute-start.2 = (bf16[392,512]{1,0:T(8,128)(2,1)}, bf16[392,512]{1,0:T(8,128)(2,1)S(1)}, u32[]{:S(2)}, u32[]{:S(2)}) collective-permute-start(bf16[392,512]{1,0:T(8,128)(2,1)} %get-tuple-element.7.y0_ref), channel_id=1, source_target_pairs={{0,16},{16,0},{1,17},{17,1},{2,18},{18,2},{3,19},{19,3},{4,20},{20... | collective-permute-start | bytes 1204232 | tf_op jit(solution)/shard_map/ppermute | solution.py:186
  57.9 1.5 %collective-permute-done.5.up_ref = bf16[392,512]{1,0:T(8,128)(2,1)S(1)} collective-permute-done((bf16[392,512]{1,0:T(8,128)(2,1)}, bf16[392,512]{1,0:T(8,128)(2,1)S(1)}, u32[]{:S(2)}, u32[]{:S(2)}) %collective-permute-start.5) | collective-permute-done | bytes 401440 | tf_op jit(solution)/shard_map/ppermute | solution.py:189
  59.4 1.9 %collective-permute-start.6 = (bf16[392,512]{1,0:T(8,128)(2,1)S(1)}, bf16[392,512]{1,0:T(8,128)(2,1)S(1)}, u32[]{:S(2)}, u32[]{:S(2)}) collective-permute-start(bf16[392,512]{1,0:T(8,128)(2,1)S(1)} %collective-permute-done.5.up_ref), channel_id=1, source_target_pairs={{0,16},{16,0},{1,17},{17,1},{2,18},{18,2},{3,19},{19,3},{4,20},{20... | collective-permute-start | bytes 1204232 | tf_op jit(solution)/shard_map/ppermute | solution.py:186
  61.3 2.4 %collective-permute-start.4 = (bf16[392,512]{1,0:T(8,128)(2,1)S(1)}, bf16[392,512]{1,0:T(8,128)(2,1)S(1)}, u32[]{:S(2)}, u32[]{:S(2)}) collective-permute-start(bf16[392,512]{1,0:T(8,128)(2,1)S(1)} %collective-permute-done.3.dn_ref), channel_id=1, source_target_pairs={{0,16},{16,0},{1,17},{17,1},{2,18},{18,2},{3,19},{19,3},{4,20},{20... | collective-permute-start | bytes 1204232 | tf_op jit(solution)/shard_map/ppermute | solution.py:186
  63.8 5.7 %collective-permute-start.7 = (bf16[192,512]{1,0:T(8,128)(2,1)}, bf16[192,512]{1,0:T(8,128)(2,1)S(1)}, u32[]{:S(2)}, u32[]{:S(2)}) collective-permute-start(bf16[192,512]{1,0:T(8,128)(2,1)} %get-tuple-element.8), channel_id=1, source_target_pairs={{0,4},{2,6},{4,8},{6,10},{8,12},{10,14},{12,0},{14,2},{1,5},{3,7},... | collective-permute-start | bytes 589832 | tf_op jit(solution)/shard_map/ppermute | solution.py:189
  69.4 1.9 %collective-permute-start.10 = (bf16[200,512]{1,0:T(8,128)(2,1)S(1)}, bf16[200,512]{1,0:T(8,128)(2,1)S(1)}, u32[]{:S(2)}, u32[]{:S(2)}) collective-permute-start(bf16[200,512]{1,0:T(8,128)(2,1)S(1)} %collective-permute-done.9.up2_ref), channel_id=1, source_target_pairs={{0,16},{16,0},{1,17},{17,1},{2,18},{18,2},{3,19},{19,3},{4,20},{20... | collective-permute-start | bytes 614408 | tf_op jit(solution)/shard_map/ppermute | solution.py:186
  71.4 11.2 %collective-permute-done.7.dn2_ref = bf16[192,512]{1,0:T(8,128)(2,1)S(1)} collective-permute-done((bf16[192,512]{1,0:T(8,128)(2,1)}, bf16[192,512]{1,0:T(8,128)(2,1)S(1)}, u32[]{:S(2)}, u32[]{:S(2)}) %collective-permute-start.7) | collective-permute-done | bytes 196640 | tf_op jit(solution)/shard_map/ppermute | solution.py:189
  82.6 1.9 %collective-permute-start.8 = (bf16[192,512]{1,0:T(8,128)(2,1)S(1)}, bf16[192,512]{1,0:T(8,128)(2,1)S(1)}, u32[]{:S(2)}, u32[]{:S(2)}) collective-permute-start(bf16[192,512]{1,0:T(8,128)(2,1)S(1)} %collective-permute-done.7.dn2_ref), channel_id=1, source_target_pairs={{0,16},{16,0},{1,17},{17,1},{2,18},{18,2},{3,19},{19,3},{4,20},{20... | collective-permute-start | bytes 589832 | tf_op jit(solution)/shard_map/ppermute | solution.py:186
  84.5 1.4 %collective-permute-done.8.dn2o_ref = bf16[192,512]{1,0:T(8,128)(2,1)S(1)} collective-permute-done((bf16[192,512]{1,0:T(8,128)(2,1)S(1)}, bf16[192,512]{1,0:T(8,128)(2,1)S(1)}, u32[]{:S(2)}, u32[]{:S(2)}) %collective-permute-start.8) | collective-permute-done | bytes 196640 | tf_op jit(solution)/shard_map/ppermute | solution.py:186
  86.0 0.6 copy-done.11
  86.6 0.1 copy-done.5
  86.7 0.1 copy-done.9
  86.8 0.1 copy-done.6
  86.9 0.7 copy-done.7
  87.7 8.9 %loss_and_grad.1 = (bf16[24,2,8,512]{3,2,1,0:T(8,128)(2,1)}, f32[1,384]{1,0:T(1,128)}) custom-call(s32[1]{0:T(128)} %bitcast.core_ref, bf16[24,2,8,512]{3,2,1,0:T(8,128)(2,1)} %bitcast.6, s32[1,384]{1,0:T(1,128)} %copy-done.2, s32[1,384]{1,0:T(1,128)} %copy-done.1, bf16[392,512]{1,0:T(8,128)(2,1)} %get-tuple-element.7.y0_ref, bf16[392,512]{1,0:T(8,128)(2,1)} %copy-done.5, ...), custom_call_target="tpu_custom_call" | custom-call | flops 4000000000 | bytes 10000000 | tf_op jit(solution)/shard_map/loss_and_grad/pallas_call | solution.py:218
  96.6 4.9 %all-to-all-start.1 = ((bf16[48,8,512]{2,1,0:T(8,128)(2,1)}), bf16[48,8,512]{2,1,0:T(8,128)(2,1)S(1)}, u32[]{:S(2)}, u32[]{:S(2)}) async-start(bf16[48,8,512]{2,1,0:T(8,128)(2,1)} %bitcast.9), calls=%async_computation.1 | async-start | bytes 786432 | tf_op jit(solution)/shard_map/all_to_all | solution.py:240
  101.5 0.6 copy-done.13
  102.1 0.6 collective-permute-start.11
  102.8 20.8 %all-to-all-done.1 = bf16[48,8,512]{2,1,0:T(8,128)(2,1)S(1)} async-done(((bf16[48,8,512]{2,1,0:T(8,128)(2,1)}), bf16[48,8,512]{2,1,0:T(8,128)(2,1)S(1)}, u32[]{:S(2)}, u32[]{:S(2)}) %all-to-all-start.1) | async-done | bytes 393248 | tf_op jit(solution)/shard_map/all_to_all | solution.py:240
  123.6 0.7 copy.6
  124.3 0.6 copy.7
  (28 shorter events, 0.1 us)
Async XLA Ops:
  0.6 18.3 %copy-start.12 = (s32[1,384]{1,0:T(1,128)S(1)}, s32[1,384]{1,0:T(1,128)}, u32[]{:S(2)}) copy-start(s32[1,384]{1,0:T(1,128)} %param.3) | copy-start | bytes 4612
  0.6 40.1 %all-to-all-start = ((bf16[48,8,512]{2,1,0:T(8,128)(2,1)}), bf16[48,8,512]{2,1,0:T(8,128)(2,1)S(1)}, u32[]{:S(2)}, u32[]{:S(2)}) async-start(bf16[48,8,512]{2,1,0:T(8,128)(2,1)} %bitcast.8), calls=%async_computation | async-start | bytes 786432 | tf_op jit(solution)/shard_map/all_to_all | solution.py:191
  19.0 20.7 %collective-permute-start.1 = (s32[1,384]{1,0:T(1,128)S(1)}, s32[1,384]{1,0:T(1,128)S(1)}, u32[]{:S(2)}, u32[]{:S(2)}) collective-permute-start(s32[1,384]{1,0:T(1,128)S(1)} %copy-done.12), channel_id=1, source_target_pairs={{0,16},{16,17},{1,0},{17,1},{2,18},{18,19},{3,2},{19,3},{4,20},{20... | collective-permute-start | bytes 4616 | tf_op jit(solution)/shard_map/ppermute | solution.py:183
  20.9 18.8 %collective-permute-start = (s32[1,384]{1,0:T(1,128)S(1)}, s32[1,384]{1,0:T(1,128)S(1)}, u32[]{:S(2)}, u32[]{:S(2)}) collective-permute-start(s32[1,384]{1,0:T(1,128)S(1)} %copy-done.12), channel_id=1, source_target_pairs={{0,0},{16,1},{1,16},{17,17},{2,2},{18,3},{3,18},{19,19},{4,4},{20,... | collective-permute-start | bytes 4616 | tf_op jit(solution)/shard_map/ppermute | solution.py:182
  39.6 1.1 copy-start.1
  39.6 1.1 copy-start.2
  40.7 0.7 copy-start
  43.6 15.8 %collective-permute-start.5 = (bf16[392,512]{1,0:T(8,128)(2,1)}, bf16[392,512]{1,0:T(8,128)(2,1)S(1)}, u32[]{:S(2)}, u32[]{:S(2)}) collective-permute-start(bf16[392,512]{1,0:T(8,128)(2,1)} %get-tuple-element.7.y0_ref), channel_id=1, source_target_pairs={{0,14},{2,0},{4,2},{6,4},{8,6},{10,8},{12,10},{14,12},{1,15},{3,1}... | collective-permute-start | bytes 1204232 | tf_op jit(solution)/shard_map/ppermute | solution.py:189
  46.0 15.4 %collective-permute-start.3 = (bf16[392,512]{1,0:T(8,128)(2,1)}, bf16[392,512]{1,0:T(8,128)(2,1)S(1)}, u32[]{:S(2)}, u32[]{:S(2)}) collective-permute-start(bf16[392,512]{1,0:T(8,128)(2,1)} %get-tuple-element.7.y0_ref), channel_id=1, source_target_pairs={{0,2},{2,4},{4,6},{6,8},{8,10},{10,12},{12,14},{14,0},{1,3},{3,5},... | collective-permute-start | bytes 1204232 | tf_op jit(solution)/shard_map/ppermute | solution.py:189
  49.5 20.0 %collective-permute-start.9 = (bf16[200,512]{1,0:T(8,128)(2,1)}, bf16[200,512]{1,0:T(8,128)(2,1)S(1)}, u32[]{:S(2)}, u32[]{:S(2)}) collective-permute-start(bf16[200,512]{1,0:T(8,128)(2,1)} %get-tuple-element.9), channel_id=1, source_target_pairs={{0,12},{2,14},{4,0},{6,2},{8,4},{10,6},{12,8},{14,10},{1,13},{3,15... | collective-permute-start | bytes 614408 | tf_op jit(solution)/shard_map/ppermute | solution.py:189
  55.9 30.0 %collective-permute-start.2 = (bf16[392,512]{1,0:T(8,128)(2,1)}, bf16[392,512]{1,0:T(8,128)(2,1)S(1)}, u32[]{:S(2)}, u32[]{:S(2)}) collective-permute-start(bf16[392,512]{1,0:T(8,128)(2,1)} %get-tuple-element.7.y0_ref), channel_id=1, source_target_pairs={{0,16},{16,0},{1,17},{17,1},{2,18},{18,2},{3,19},{19,3},{4,20},{20... | collective-permute-start | bytes 1204232 | tf_op jit(solution)/shard_map/ppermute | solution.py:186
  59.4 26.6 %copy-start.3 = (bf16[392,512]{1,0:T(8,128)(2,1)}, bf16[392,512]{1,0:T(8,128)(2,1)S(1)}, u32[]{:S(2)}) copy-start(bf16[392,512]{1,0:T(8,128)(2,1)S(1)} %collective-permute-done.5.up_ref) | copy-start | bytes 1204228
  59.4 26.5 %collective-permute-start.6 = (bf16[392,512]{1,0:T(8,128)(2,1)S(1)}, bf16[392,512]{1,0:T(8,128)(2,1)S(1)}, u32[]{:S(2)}, u32[]{:S(2)}) collective-permute-start(bf16[392,512]{1,0:T(8,128)(2,1)S(1)} %collective-permute-done.5.up_ref), channel_id=1, source_target_pairs={{0,16},{16,0},{1,17},{17,1},{2,18},{18,2},{3,19},{19,3},{4,20},{20... | collective-permute-start | bytes 1204232 | tf_op jit(solution)/shard_map/ppermute | solution.py:186
  61.3 24.6 %copy-start.4 = (bf16[392,512]{1,0:T(8,128)(2,1)}, bf16[392,512]{1,0:T(8,128)(2,1)S(1)}, u32[]{:S(2)}) copy-start(bf16[392,512]{1,0:T(8,128)(2,1)S(1)} %collective-permute-done.3.dn_ref) | copy-start | bytes 1204228
  61.3 24.6 %collective-permute-start.4 = (bf16[392,512]{1,0:T(8,128)(2,1)S(1)}, bf16[392,512]{1,0:T(8,128)(2,1)S(1)}, u32[]{:S(2)}, u32[]{:S(2)}) collective-permute-start(bf16[392,512]{1,0:T(8,128)(2,1)S(1)} %collective-permute-done.3.dn_ref), channel_id=1, source_target_pairs={{0,16},{16,0},{1,17},{17,1},{2,18},{18,2},{3,19},{19,3},{4,20},{20... | collective-permute-start | bytes 1204232 | tf_op jit(solution)/shard_map/ppermute | solution.py:186
  63.8 18.8 %collective-permute-start.7 = (bf16[192,512]{1,0:T(8,128)(2,1)}, bf16[192,512]{1,0:T(8,128)(2,1)S(1)}, u32[]{:S(2)}, u32[]{:S(2)}) collective-permute-start(bf16[192,512]{1,0:T(8,128)(2,1)} %get-tuple-element.8), channel_id=1, source_target_pairs={{0,4},{2,6},{4,8},{6,10},{8,12},{10,14},{12,0},{14,2},{1,5},{3,7},... | collective-permute-start | bytes 589832 | tf_op jit(solution)/shard_map/ppermute | solution.py:189
  69.4 16.6 %copy-start.8 = (bf16[200,512]{1,0:T(8,128)(2,1)}, bf16[200,512]{1,0:T(8,128)(2,1)S(1)}, u32[]{:S(2)}) copy-start(bf16[200,512]{1,0:T(8,128)(2,1)S(1)} %collective-permute-done.9.up2_ref) | copy-start | bytes 614404
  69.4 16.5 %collective-permute-start.10 = (bf16[200,512]{1,0:T(8,128)(2,1)S(1)}, bf16[200,512]{1,0:T(8,128)(2,1)S(1)}, u32[]{:S(2)}, u32[]{:S(2)}) collective-permute-start(bf16[200,512]{1,0:T(8,128)(2,1)S(1)} %collective-permute-done.9.up2_ref), channel_id=1, source_target_pairs={{0,16},{16,0},{1,17},{17,1},{2,18},{18,2},{3,19},{19,3},{4,20},{20... | collective-permute-start | bytes 614408 | tf_op jit(solution)/shard_map/ppermute | solution.py:186
  82.6 3.4 %copy-start.10 = (bf16[192,512]{1,0:T(8,128)(2,1)}, bf16[192,512]{1,0:T(8,128)(2,1)S(1)}, u32[]{:S(2)}) copy-start(bf16[192,512]{1,0:T(8,128)(2,1)S(1)} %collective-permute-done.7.dn2_ref) | copy-start | bytes 589828
  82.6 3.3 %collective-permute-start.8 = (bf16[192,512]{1,0:T(8,128)(2,1)S(1)}, bf16[192,512]{1,0:T(8,128)(2,1)S(1)}, u32[]{:S(2)}, u32[]{:S(2)}) collective-permute-start(bf16[192,512]{1,0:T(8,128)(2,1)S(1)} %collective-permute-done.7.dn2_ref), channel_id=1, source_target_pairs={{0,16},{16,0},{1,17},{17,1},{2,18},{18,2},{3,19},{19,3},{4,20},{20... | collective-permute-start | bytes 589832 | tf_op jit(solution)/shard_map/ppermute | solution.py:186
  85.9 0.7 copy-start.11
  85.9 0.8 copy-start.5
  85.9 0.9 copy-start.9
  85.9 1.0 copy-start.6
  86.9 0.7 copy-start.7
  96.6 27.0 %all-to-all-start.1 = ((bf16[48,8,512]{2,1,0:T(8,128)(2,1)}), bf16[48,8,512]{2,1,0:T(8,128)(2,1)S(1)}, u32[]{:S(2)}, u32[]{:S(2)}) async-start(bf16[48,8,512]{2,1,0:T(8,128)(2,1)} %bitcast.9), calls=%async_computation.1 | async-start | bytes 786432 | tf_op jit(solution)/shard_map/all_to_all | solution.py:240
  101.5 0.6 copy-start.13
  102.1 0.7 collective-permute-start.11
